TPU v7x, 512 devices: a whole 4x8x8 slice. The times are simulated.
512 devices in a mesh: freq: 16 (over y, core), offset: 32 (over x, z).
Axes of the slice: x: 4, y: 8, z: 8, core: 2. Of those that a mesh axis runs over, the one named last changes fastest.
Arguments:
- raw_traces: bfloat16 [32768, 2048], P('offset', 'freq'), may hold values from -6 to 6
- trace_slot: int32 [32, 1024], P(None, 'offset'), may hold values from 0 to 1023, as said below
- offset_index: int32 [1024], replicated, may hold values from 1 to 1023
- slowness_index: int32 [256], replicated, may hold values from 0 to 511
Outputs:
- radon: float32 [256, 1024, 64], P('offset', 'freq')
Inputs may be any that keep to these rules, and one draw needn't show every extreme that they name: `trace_slot`: in every aligned block of 32 columns, the 32 x 32 entries name each of 0 to 1023 exactly once.
All inputs are finite; a program needn't handle non-finite values.
Results may differ from a plain program's by a relative error of at most 0.0046.
Values may be sent and summed in bfloat16 or wider, within the bound.
A program may use at most 64 MiB of HBM per device.

v0:
```python
import math
import jax
import jax.numpy as jnp
from jax import lax
from jax.sharding import Mesh
from jax.sharding import PartitionSpec as P

NF = 1024
OFFSET = ("offset_0", "offset_1")
APEX_TIME = 100.0
CURVATURE = 0.0003


def own_rows(total, axes):
    for axis in axes:
        total = lax.psum_scatter(total, axis, scatter_dimension=0, tiled=True)
    return total


def moveout(slowness, offset_grid):
    spread = (
        CURVATURE * slowness.astype(jnp.float32)[:, None] * offset_grid.astype(jnp.float32)[None, :]
    )
    return jnp.sqrt(APEX_TIME * APEX_TIME + spread * spread) - APEX_TIME


def whole_table(local_freqs, total_time):
    column_total = 2 * NF
    column = jnp.arange(column_total, dtype=jnp.int32)
    band_ids = column // (2 * local_freqs)
    within = column % (2 * local_freqs)
    freq_ids = band_ids * local_freqs + within % local_freqs
    shifts = jnp.where(within < local_freqs, 0, total_time // 2).astype(jnp.int32)
    odd_rates = 2 * freq_ids + 1
    fine_size = 64
    coarse_size = total_time // fine_size
    period = 2 * total_time
    coarse_ids = jnp.arange(coarse_size, dtype=jnp.int32)[:, None]
    fine_ids = jnp.arange(fine_size, dtype=jnp.int32)[:, None]
    coarse_turn = coarse_ids * fine_size % period * odd_rates[None, :] % period
    fine_turn = (fine_ids * odd_rates[None, :] + shifts[None, :]) % period
    coarse_angle = coarse_turn.astype(jnp.float32) * (math.pi / total_time)
    fine_angle = fine_turn.astype(jnp.float32) * (math.pi / total_time)
    coarse_cos = jnp.cos(coarse_angle)
    coarse_sin = jnp.sin(coarse_angle)
    fine_cos = jnp.cos(fine_angle)
    fine_sin = jnp.sin(fine_angle)
    values = (
        coarse_cos[:, None, :] * fine_cos[None, :, :]
        - coarse_sin[:, None, :] * fine_sin[None, :, :]
    )
    values = values.reshape(total_time, column_total)
    return (values * (1.0 / math.sqrt(total_time))).astype(jnp.bfloat16)


def local(raw_traces, trace_slot, offset_index, slowness_index):
    gathers, local_offsets = trace_slot.shape
    local_times = raw_traces.shape[1]
    freq_devices = lax.axis_size("freq")
    offset_devices = lax.axis_size(OFFSET)
    total_time = local_times * freq_devices
    local_freqs = NF // freq_devices
    trace_rows = gathers * local_offsets
    picked = raw_traces[trace_slot.reshape(-1)]
    grouped = picked.reshape(freq_devices, trace_rows // freq_devices, local_times)
    fourier_table = whole_table(local_freqs, total_time)
    series = lax.all_to_all(grouped, "freq", split_axis=0, concat_axis=2, tiled=True)
    flattened = series.reshape(series.shape[1], total_time)
    spectrum = jnp.dot(flattened, fourier_table, preferred_element_type=jnp.float32).astype(
        jnp.bfloat16
    )
    spectrum = jnp.transpose(
        spectrum.reshape(flattened.shape[0], freq_devices, 2 * local_freqs), (1, 0, 2)
    )
    assembled = lax.all_to_all(spectrum, "freq", split_axis=0, concat_axis=0, tiled=True)
    spectra = assembled.reshape(gathers, local_offsets, 2 * local_freqs)
    real_part = spectra[:, :, :local_freqs]
    imag_part = spectra[:, :, local_freqs:]
    freq_ids = lax.axis_index("freq") * local_freqs + jnp.arange(local_freqs, dtype=jnp.int32)
    angular = (2 * freq_ids + 1).astype(jnp.float32) * (math.pi / total_time)
    own_offsets = lax.dynamic_slice_in_dim(
        offset_index, lax.axis_index(OFFSET) * local_offsets, local_offsets
    )
    delays = moveout(slowness_index, own_offsets)
    phases = angular[:, None, None] * delays[None, :, :]
    cosine = jnp.cos(phases).astype(jnp.bfloat16)
    sines = jnp.sin(phases).astype(jnp.bfloat16)
    real_out = jnp.einsum(
        "fph,ghf->pfg", cosine, real_part, preferred_element_type=jnp.float32
    ) - jnp.einsum("fph,ghf->pfg", sines, imag_part, preferred_element_type=jnp.float32)
    imag_out = jnp.einsum(
        "fph,ghf->pfg", sines, real_part, preferred_element_type=jnp.float32
    ) + jnp.einsum("fph,ghf->pfg", cosine, imag_part, preferred_element_type=jnp.float32)
    summed = own_rows(jnp.concatenate([real_out, imag_out], axis=2), OFFSET)
    return summed * (1.0 / math.sqrt(local_offsets * offset_devices))


def solution(mesh):
    torus = Mesh(mesh.devices.reshape(mesh.shape["freq"], 4, 8), ("freq", "offset_0", "offset_1"))
    placed = (P(OFFSET, "freq"), P(None, OFFSET), P(), P())
    return jax.shard_map(
        local, mesh=torus, in_specs=placed, out_specs=P(OFFSET, "freq", None), check_vma=False
    )
```

profile of v0, /device:TPU:8, one launch (start us, length us, event | category | flops | bytes accessed | tf_op | source)
XLA Modules:
  0.0 206.7 jit_solution(16207781302193923566)
XLA Ops:
  6.5 0.0 copy-start
  6.5 0.8 reshape.308
  7.4 0.1 copy-done
  7.5 4.3 %gather_fusion = bf16[1024,128]{1,0:T(8,128)(2,1)} fusion(bf16[1024,128]{1,0:T(8,128)(2,1)S(1)} %copy-done, s32[1024]{0:T(1024)S(1)} %broadcast_clamp_fusion), kind=kCustom, calls=%fused_computation | custom fusion | bytes 528384 | tf_op jit(solution)/shard_map/gather | solution.py:64
  11.8 9.1 %all-to-all-start = ((bf16[16,64,128]{2,1,0:T(8,128)(2,1)}), bf16[16,64,128]{2,1,0:T(8,128)(2,1)S(1)}, u32[]{:S(2)}, u32[]{:S(2)}) async-start(bf16[16,64,128]{2,1,0:T(8,128)(2,1)} %bitcast.1), calls=%async_computation | async-start | bytes 524288 | tf_op jit(solution)/shard_map/all_to_all | solution.py:67
  21.0 2.1 fusion.21
  23.0 1.1 fusion.28
  24.1 6.2 %multiply_convert_fusion = bf16[32,64,2048]{2,1,0:T(8,128)(2,1)} fusion(f32[64,2048]{1,0:T(8,128)S(1)} %get-tuple-element.8, f32[32,2048]{1,0:T(8,128)S(1)} %get-tuple-element.10, f32[64,2048]{1,0:T(8,128)S(1)} %get-tuple-element.7, f32[32,2048]{1,0:T(8,128)S(1)} %get-tuple-element.9), kind=kLoop, calls=%fused_computation.1 | loop fusion | flops 20971520 | bytes 9961472 | tf_op jit(solution)/shard_map/convert_element_type | solution.py:53
  30.3 0.3 all-to-all-done
  30.6 0.2 copy.12
  30.8 0.0 copy-start.1
  30.8 5.0 %fusion.8 = bf16[8,16,8,128]{3,2,1,0:T(8,128)(2,1)S(1)} fusion(bf16[2048,2048]{1,0:T(8,128)(2,1)} %bitcast.32, bf16[8,8,16,128]{3,2,1,0:T(8,128)(2,1)S(1)} %bitcast.36), kind=kOutput, calls=%fused_computation.12 | convolution fusion | flops 537001984 | bytes 8912896 | tf_op jit(solution)/shard_map/dot_general | solution.py:69
  35.7 0.8 copy.30
  36.5 7.0 %all-to-all-start.1 = ((bf16[16,64,128]{2,1,0:T(8,128)(2,1)}), bf16[16,64,128]{2,1,0:T(8,128)(2,1)S(1)}, u32[]{:S(2)}, u32[]{:S(2)}) async-start(bf16[16,64,128]{2,1,0:T(8,128)(2,1)} %bitcast.31), calls=%async_computation.1 | async-start | bytes 524288 | tf_op jit(solution)/shard_map/all_to_all | solution.py:75
  43.5 0.2 reduce-scatter.7.cloned.1.call-start
  43.7 0.8 dynamic-slice_convert_fusion
  44.5 0.0 copy-done.1
  44.5 0.1 sqrt_add_fusion
  44.6 8.5 %all-to-all-done.1 = bf16[16,64,128]{2,1,0:T(8,128)(2,1)S(1)} async-done(((bf16[16,64,128]{2,1,0:T(8,128)(2,1)}), bf16[16,64,128]{2,1,0:T(8,128)(2,1)S(1)}, u32[]{:S(2)}, u32[]{:S(2)}) %all-to-all-start.1) | async-done | bytes 262176 | tf_op jit(solution)/shard_map/all_to_all | solution.py:75
  53.1 0.1 fusion.44
  53.3 0.8 copy.21
  54.0 8.5 %fusion.2 = f32[64,32,256]{2,1,0:T(8,128)} fusion(bf16[32,32,64]{1,0,2:T(8,128)(2,1)S(1)} %copy.21, f32[256,32]{0,1:T(8,128)S(1)} %sqrt_add_fusion, f32[64]{0:T(128)S(1)} %convert_multiply_fusion.1), kind=kOutput, calls=%fused_computation.10 | convolution fusion | flops 34603008 | bytes 2261248 | tf_op jit(solution)/shard_map/fph,ghf->pfg/dot_general | solution.py:91
  62.5 6.9 %fusion.6 = f32[64,32,256]{2,1,0:T(8,128)S(1)} fusion(bf16[32,32,64]{1,0,2:T(8,128)(2,1)S(1)} %copy.21, f32[256,32]{0,1:T(8,128)S(1)} %sqrt_add_fusion, f32[64]{0:T(128)S(1)} %convert_multiply_fusion.1), kind=kOutput, calls=%fused_computation.11 | convolution fusion | flops 34603008 | bytes 2261248 | tf_op jit(solution)/shard_map/fph,ghf->pfg/dot_general | solution.py:88
  69.4 0.8 copy.22
  70.2 9.6 %add_bitcast_fusion = f32[256,64,32]{0,2,1:T(8,128)S(1)} fusion(f32[64,32,256]{2,1,0:T(8,128)} %fusion.2, bf16[32,32,64]{1,0,2:T(8,128)(2,1)S(1)} %copy.22, f32[256,32]{0,1:T(8,128)S(1)} %sqrt_add_fusion, f32[64]{0:T(128)S(1)} %convert_multiply_fusion.1), kind=kOutput, calls=%fused_computation.8 | convolution fusion | flops 35127296 | bytes 4358400 | tf_op jit(solution)/shard_map/fph,ghf->pfg/dot_general | solution.py:93
  79.8 7.0 %subtract_bitcast_fusion = f32[256,64,32]{0,2,1:T(8,128)S(1)} fusion(f32[64,32,256]{2,1,0:T(8,128)S(1)} %fusion.6, bf16[32,32,64]{1,0,2:T(8,128)(2,1)S(1)} %copy.22, f32[256,32]{0,1:T(8,128)S(1)} %sqrt_add_fusion, f32[64]{0:T(128)S(1)} %convert_multiply_fusion.1), kind=kOutput, calls=%fused_computation.9 | convolution fusion | flops 35127296 | bytes 4358400 | tf_op jit(solution)/shard_map/fph,ghf->pfg/dot_general | solution.py:90
  86.8 2.2 %pad_maximum_fusion = f32[256,64,64]{0,2,1:T(8,128)} fusion(f32[256,64,32]{0,2,1:T(8,128)S(1)} %add_bitcast_fusion, f32[256,64,32]{0,2,1:T(8,128)S(1)} %subtract_bitcast_fusion), kind=kLoop, calls=%fused_computation.2 | loop fusion | flops 1048576 | bytes 8388608 | tf_op jit(solution)/shard_map/concatenate | solution.py:94
  89.0 5.6 %copy.19 = f32[256,4096]{1,0:T(8,128)} copy(f32[256,4096]{0,1:T(8,128)} %bitcast.33) | data formatting | bytes 8388608
  94.7 0.0 reduce-scatter.7.cloned.1.call-update
  94.7 0.0 reduce-scatter.5.cloned.1.call-start
  94.7 52.6 %reduce-scatter.7.cloned.1.call-done = f32[64,4096]{1,0:T(8,128)} async-done(((f32[256,4096]{1,0:T(8,128)}), f32[64,4096]{1,0:T(8,128)}) %reduce-scatter.7.cloned.1.call-update) | async-done | bytes 1048592
  147.4 1.8 copy.20
  149.2 2.7 %copy.16 = f32[64,64,64]{2,1,0:T(8,128)} copy(f32[64,64,64]{0,2,1:T(8,128)S(1)} %bitcast.34) | data formatting | bytes 2097152 | tf_op jit(solution)/shard_map/reduce_scatter | solution.py:16
  151.9 0.0 reduce-scatter.5.cloned.1.call-update
  151.9 46.2 %reduce-scatter.5.cloned.1.call-done = f32[8,64,64]{2,1,0:T(8,128)} async-done(((f32[64,64,64]{2,1,0:T(8,128)}), f32[8,64,64]{2,1,0:T(8,128)}) %reduce-scatter.5.cloned.1.call-update) | async-done | bytes 131088 | tf_op jit(solution)/shard_map/reduce_scatter | solution.py:16
  198.1 1.7 broadcast_multiply_fusion
  (6 shorter events, 0.0 us)
Async XLA Ops:
  6.5 1.0 copy-start
  11.8 18.8 %all-to-all-start = ((bf16[16,64,128]{2,1,0:T(8,128)(2,1)}), bf16[16,64,128]{2,1,0:T(8,128)(2,1)S(1)}, u32[]{:S(2)}, u32[]{:S(2)}) async-start(bf16[16,64,128]{2,1,0:T(8,128)(2,1)} %bitcast.1), calls=%async_computation | async-start | bytes 524288 | tf_op jit(solution)/shard_map/all_to_all | solution.py:67
  30.8 13.7 %copy-start.1 = (s32[256]{0:T(256)S(1)}, s32[256]{0:T(256)}, u32[]{:S(2)}) copy-start(s32[256]{0:T(256)} %param.7) | copy-start | bytes 3076
  36.5 16.6 %all-to-all-start.1 = ((bf16[16,64,128]{2,1,0:T(8,128)(2,1)}), bf16[16,64,128]{2,1,0:T(8,128)(2,1)S(1)}, u32[]{:S(2)}, u32[]{:S(2)}) async-start(bf16[16,64,128]{2,1,0:T(8,128)(2,1)} %bitcast.31), calls=%async_computation.1 | async-start | bytes 524288 | tf_op jit(solution)/shard_map/all_to_all | solution.py:75
  43.5 103.9 %reduce-scatter.7.cloned.1.call-start = ((), (), s32[]{:S(2)}) async-start(), calls=%async_computation.5 | async-start | bytes 5242880
  94.7 103.5 %reduce-scatter.5.cloned.1.call-start = ((), (), s32[]{:S(2)}) async-start(), calls=%async_computation.4 | async-start | bytes 2359296 | tf_op jit(solution)/shard_map/reduce_scatter | solution.py:16
Sparse Core Ops, SparseCore 0:
  94.8 52.5 reduce-scatter.6
  152.1 46.0 reduce-scatter.4
where the time goes:
time: 207 us
  waiting for transfers between devices  108 us (52%)
  matrix products  36.9 us (18%)
  local copies, waits for them, and re-layouts  18.1 us (9%)
  starting transfers between devices  16.4 us (8%)
  other arithmetic  14.1 us (7%)
  between operations  13.5 us (7%)
    unnamed x3, waiting for transfers between devices  52.7 us
    reduce_scatter x1, waiting for transfers between devices, own_rows(): total = lax.psum_scatter(total, axis, scatter_dimension=0, tiled=True)  46.2 us
    dot_general x1, matrix products, local(): jnp.einsum('fph,ghf->pfg', cosine, imag_part, preferred_element_type=jnp....  9.6 us
    all_to_all x1, starting transfers between devices, local(): lax.all_to_all(grouped, 'freq', split_axis=0, concat_axis=2, tiled=True)  9.12 us
    unnamed x8, local copies, waits for them, and re-layouts  9.12 us
    all_to_all x1, waiting for transfers between devices, local(): lax.all_to_all(spectrum, 'freq', split_axis=0, concat_axis=0, tiled=True)  8.5 us
    dot_general x1, matrix products, local(): jnp.einsum('fph,ghf->pfg', sines, real_part, preferred_element_type=jnp.f...  8.45 us
    dot_general x1, matrix products, local(): jnp.einsum('fph,ghf->pfg', sines, imag_part, preferred_element_type=jnp.f...  7.03 us
  transfers between devices with their start and end apart: 4, of which 4 were waited for; matrix products, arithmetic and copies ran while one was open for 5% of the time, Pallas kernels for 0%

commit v1 on v0

--- a/solution.py
+++ b/solution.py
@@ -1,3 +1,4 @@
+import functools
 import math
 import jax
 import jax.numpy as jnp
@@ -9,6 +10,37 @@
 OFFSET = ("offset_0", "offset_1")
 APEX_TIME = 100.0
 CURVATURE = 0.0003
+
+
+def watch_clusters(array_in, d_out, mine):
+    heard = array_in.shape
+    return jnp.moveaxis(
+        array_in.reshape(*heard[:d_out], mine, heard[d_out] // mine, *heard[d_out + 1 :]), d_out, 0
+    )
+
+
+def assign_core(z_in, along_dim):
+    z_in = jnp.moveaxis(z_in, 0, along_dim)
+    z1 = z_in.shape
+    return z_in.reshape(*z1[:along_dim], z1[along_dim] * z1[along_dim + 1], *z1[along_dim + 2 :])
+
+
+def push_strips_all_now(original, shard_axis, local_array, u_in):
+    side_arr, formed = (lax.axis_size(shard_axis), lax.axis_index(shard_axis))
+    base_arr = watch_clusters(original, local_array, side_arr)
+    found = [base_arr[formed]]
+    for kk in range(1, side_arr):
+        e_now = base_arr[formed ^ kk]
+        found.append(
+            lax.ppermute(
+                e_now, axis_name=shard_axis, perm=[(nth, nth ^ kk) for nth in range(side_arr)]
+            )
+        )
+    base_arr = jnp.stack(found)[formed ^ jnp.arange(side_arr)]
+    return assign_core(base_arr, u_in)
+
+
+move_values = functools.partial(push_strips_all_now, shard_axis="freq", local_array=0, u_in=0)
 
 
 def own_rows(total, axes):
@@ -72,7 +104,7 @@
     spectrum = jnp.transpose(
         spectrum.reshape(flattened.shape[0], freq_devices, 2 * local_freqs), (1, 0, 2)
     )
-    assembled = lax.all_to_all(spectrum, "freq", split_axis=0, concat_axis=0, tiled=True)
+    assembled = move_values(spectrum)
     spectra = assembled.reshape(gathers, local_offsets, 2 * local_freqs)
     real_part = spectra[:, :, :local_freqs]
     imag_part = spectra[:, :, local_freqs:]

time: 207 us -> 253 us (1.22)
  the two profiles are of different devices: /device:TPU:8 before, /device:TPU:2 now
where the time goes in v1:
time: 253 us; the launch traced here: 252 us
  waiting for transfers between devices  106 us (42%)
  starting transfers between devices  61.7 us (24%)
  matrix products  36.9 us (15%)
  local copies, waits for them, and re-layouts  19 us (8%)
  other arithmetic  14.2 us (6%)
  between operations  14 us (6%)
    unnamed x3, waiting for transfers between devices  54.8 us
    ppermute x15, starting transfers between devices, push_strips_all_now(): lax.ppermute(e_now, axis_name=shard_axis, perm=[(nth, nth ^ kk) for nth i...  54.4 us
    reduce_scatter x1, waiting for transfers between devices, own_rows(): total = lax.psum_scatter(total, axis, scatter_dimension=0, tiled=True)  47.5 us
    dot_general x1, matrix products, local(): jnp.einsum('fph,ghf->pfg', cosine, imag_part, preferred_element_type=jnp....  9.6 us
    unnamed x39, local copies, waits for them, and re-layouts  9.41 us
    dot_general x1, matrix products, local(): jnp.einsum('fph,ghf->pfg', sines, real_part, preferred_element_type=jnp.f...  8.46 us
    all_to_all x1, starting transfers between devices, local(): lax.all_to_all(grouped, 'freq', split_axis=0, concat_axis=2, tiled=True)  7.21 us
    dot_general x1, matrix products, local(): jnp.einsum('fph,ghf->pfg', sines, imag_part, preferred_element_type=jnp.f...  7.03 us
  transfers between devices with their start and end apart: 18, of which 5 were waited for; matrix products, arithmetic and copies ran while one was open for 4% of the time, Pallas kernels for 0%

profile of v1, /device:TPU:2, one launch (start us, length us, event | category | flops | bytes accessed | tf_op | source)
XLA Modules:
  0.0 252.0 jit_solution(1820577896534052213)
XLA Ops:
  6.5 0.8 reshape.370
  7.4 0.1 copy-done
  7.5 4.3 %gather_fusion = bf16[1024,128]{1,0:T(8,128)(2,1)} fusion(bf16[1024,128]{1,0:T(8,128)(2,1)S(1)} %copy-done, s32[1024]{0:T(1024)S(1)} %broadcast_clamp_fusion), kind=kCustom, calls=%fused_computation | custom fusion | bytes 528384 | tf_op jit(solution)/shard_map/gather | solution.py:96
  11.8 7.2 %all-to-all-start = ((bf16[16,64,128]{2,1,0:T(8,128)(2,1)}), bf16[16,64,128]{2,1,0:T(8,128)(2,1)S(1)}, u32[]{:S(2)}, u32[]{:S(2)}) async-start(bf16[16,64,128]{2,1,0:T(8,128)(2,1)} %bitcast.1), calls=%async_computation | async-start | bytes 524288 | tf_op jit(solution)/shard_map/all_to_all | solution.py:99
  19.0 0.0 reduce-scatter.7.cloned.1.call-start
  19.1 2.1 fusion.21
  21.2 1.1 fusion.28
  22.3 6.2 %multiply_convert_fusion = bf16[32,64,2048]{2,1,0:T(8,128)(2,1)} fusion(f32[64,2048]{1,0:T(8,128)S(1)} %get-tuple-element.24, f32[32,2048]{1,0:T(8,128)S(1)} %get-tuple-element.26, f32[64,2048]{1,0:T(8,128)S(1)} %get-tuple-element.23, f32[32,2048]{1,0:T(8,128)S(1)} %get-tuple-element.25), kind=kLoop, calls=%fused_computation.2 | loop fusion | flops 20971520 | bytes 9961472 | tf_op jit(solution)/shard_map/convert_element_type | solution.py:85
  28.5 0.8 dynamic-slice_convert_fusion
  29.3 0.1 sqrt_add_fusion
  29.4 0.8 all-to-all-done
  30.2 0.2 copy.27
  30.3 4.9 %fusion.8 = bf16[8,8,16,128]{3,1,2,0:T(8,128)(2,1)S(1)} fusion(bf16[2048,2048]{1,0:T(8,128)(2,1)} %bitcast.111, bf16[8,8,16,128]{3,2,1,0:T(8,128)(2,1)S(1)} %bitcast.116), kind=kOutput, calls=%fused_computation.13 | convolution fusion | flops 537001984 | bytes 8912896 | tf_op jit(solution)/shard_map/dot_general | solution.py:101
  35.3 0.8 constant_dynamic-slice_fusion
  36.2 2.8 %collective-permute-start = (bf16[1,64,128]{2,1,0:T(8,128)(2,1)S(1)}, bf16[1,64,128]{2,1,0:T(8,128)(2,1)S(1)}, u32[]{:S(2)}, u32[]{:S(2)}) collective-permute-start(bf16[1,64,128]{2,1,0:T(8,128)(2,1)S(1)} %bitcast.133), channel_id=1, source_target_pairs={{0,32},{32,0},{64,96},{96,64},{128,160},{160,128},{192,224},{224,1... | collective-permute-start | bytes 49160 | tf_op jit(solution)/shard_map/ppermute | solution.py:35
  39.0 2.3 collective-permute-start.1
  41.3 2.8 %collective-permute-start.2 = (bf16[1,64,128]{2,1,0:T(8,128)(2,1)S(1)}, bf16[1,64,128]{2,1,0:T(8,128)(2,1)S(1)}, u32[]{:S(2)}, u32[]{:S(2)}) collective-permute-start(bf16[1,64,128]{2,1,0:T(8,128)(2,1)S(1)} %bitcast.131), channel_id=1, source_target_pairs={{0,96},{32,64},{64,32},{96,0},{128,224},{160,192},{192,160},{224,1... | collective-permute-start | bytes 49160 | tf_op jit(solution)/shard_map/ppermute | solution.py:35
  44.2 3.6 %collective-permute-start.3 = (bf16[1,64,128]{2,1,0:T(8,128)(2,1)S(1)}, bf16[1,64,128]{2,1,0:T(8,128)(2,1)S(1)}, u32[]{:S(2)}, u32[]{:S(2)}) collective-permute-start(bf16[1,64,128]{2,1,0:T(8,128)(2,1)S(1)} %bitcast.130), channel_id=1, source_target_pairs={{0,128},{32,160},{64,192},{96,224},{128,0},{160,32},{192,64},{224,... | collective-permute-start | bytes 49160 | tf_op jit(solution)/shard_map/ppermute | solution.py:35
  47.8 3.2 %collective-permute-start.4 = (bf16[1,64,128]{2,1,0:T(8,128)(2,1)S(1)}, bf16[1,64,128]{2,1,0:T(8,128)(2,1)S(1)}, u32[]{:S(2)}, u32[]{:S(2)}) collective-permute-start(bf16[1,64,128]{2,1,0:T(8,128)(2,1)S(1)} %bitcast.129), channel_id=1, source_target_pairs={{0,160},{32,128},{64,224},{96,192},{128,32},{160,0},{192,96},{224,... | collective-permute-start | bytes 49160 | tf_op jit(solution)/shard_map/ppermute | solution.py:35
  51.2 4.1 %collective-permute-start.5 = (bf16[1,64,128]{2,1,0:T(8,128)(2,1)S(1)}, bf16[1,64,128]{2,1,0:T(8,128)(2,1)S(1)}, u32[]{:S(2)}, u32[]{:S(2)}) collective-permute-start(bf16[1,64,128]{2,1,0:T(8,128)(2,1)S(1)} %bitcast.128), channel_id=1, source_target_pairs={{0,192},{32,224},{64,128},{96,160},{128,64},{160,96},{192,0},{224,... | collective-permute-start | bytes 49160 | tf_op jit(solution)/shard_map/ppermute | solution.py:35
  55.4 2.8 %collective-permute-start.6 = (bf16[1,64,128]{2,1,0:T(8,128)(2,1)S(1)}, bf16[1,64,128]{2,1,0:T(8,128)(2,1)S(1)}, u32[]{:S(2)}, u32[]{:S(2)}) collective-permute-start(bf16[1,64,128]{2,1,0:T(8,128)(2,1)S(1)} %bitcast.127), channel_id=1, source_target_pairs={{0,224},{32,192},{64,160},{96,128},{128,96},{160,64},{192,32},{224... | collective-permute-start | bytes 49160 | tf_op jit(solution)/shard_map/ppermute | solution.py:35
  58.2 6.6 %collective-permute-start.7 = (bf16[1,64,128]{2,1,0:T(8,128)(2,1)S(1)}, bf16[1,64,128]{2,1,0:T(8,128)(2,1)S(1)}, u32[]{:S(2)}, u32[]{:S(2)}) collective-permute-start(bf16[1,64,128]{2,1,0:T(8,128)(2,1)S(1)} %bitcast.126), channel_id=1, source_target_pairs={{0,256},{32,288},{64,320},{96,352},{128,384},{160,416},{192,448},{... | collective-permute-start | bytes 49160 | tf_op jit(solution)/shard_map/ppermute | solution.py:35
  64.9 3.2 %collective-permute-start.8 = (bf16[1,64,128]{2,1,0:T(8,128)(2,1)S(1)}, bf16[1,64,128]{2,1,0:T(8,128)(2,1)S(1)}, u32[]{:S(2)}, u32[]{:S(2)}) collective-permute-start(bf16[1,64,128]{2,1,0:T(8,128)(2,1)S(1)} %bitcast.125), channel_id=1, source_target_pairs={{0,288},{32,256},{64,352},{96,320},{128,416},{160,384},{192,480},{... | collective-permute-start | bytes 49160 | tf_op jit(solution)/shard_map/ppermute | solution.py:35
  68.2 3.5 %collective-permute-start.9 = (bf16[1,64,128]{2,1,0:T(8,128)(2,1)S(1)}, bf16[1,64,128]{2,1,0:T(8,128)(2,1)S(1)}, u32[]{:S(2)}, u32[]{:S(2)}) collective-permute-start(bf16[1,64,128]{2,1,0:T(8,128)(2,1)S(1)} %bitcast.124), channel_id=1, source_target_pairs={{0,320},{32,352},{64,256},{96,288},{128,448},{160,480},{192,384},{... | collective-permute-start | bytes 49160 | tf_op jit(solution)/shard_map/ppermute | solution.py:35
  71.7 4.6 %collective-permute-start.10 = (bf16[1,64,128]{2,1,0:T(8,128)(2,1)S(1)}, bf16[1,64,128]{2,1,0:T(8,128)(2,1)S(1)}, u32[]{:S(2)}, u32[]{:S(2)}) collective-permute-start(bf16[1,64,128]{2,1,0:T(8,128)(2,1)S(1)} %bitcast.123), channel_id=1, source_target_pairs={{0,352},{32,320},{64,288},{96,256},{128,480},{160,448},{192,416},{... | collective-permute-start | bytes 49160 | tf_op jit(solution)/shard_map/ppermute | solution.py:35
  76.4 3.0 %collective-permute-start.11 = (bf16[1,64,128]{2,1,0:T(8,128)(2,1)S(1)}, bf16[1,64,128]{2,1,0:T(8,128)(2,1)S(1)}, u32[]{:S(2)}, u32[]{:S(2)}) collective-permute-start(bf16[1,64,128]{2,1,0:T(8,128)(2,1)S(1)} %bitcast.122), channel_id=1, source_target_pairs={{0,384},{32,416},{64,448},{96,480},{128,256},{160,288},{192,320},{... | collective-permute-start | bytes 49160 | tf_op jit(solution)/shard_map/ppermute | solution.py:35
  79.5 5.0 %collective-permute-start.12 = (bf16[1,64,128]{2,1,0:T(8,128)(2,1)S(1)}, bf16[1,64,128]{2,1,0:T(8,128)(2,1)S(1)}, u32[]{:S(2)}, u32[]{:S(2)}) collective-permute-start(bf16[1,64,128]{2,1,0:T(8,128)(2,1)S(1)} %bitcast.121), channel_id=1, source_target_pairs={{0,416},{32,384},{64,480},{96,448},{128,288},{160,256},{192,352},{... | collective-permute-start | bytes 49160 | tf_op jit(solution)/shard_map/ppermute | solution.py:35
  84.5 3.5 %collective-permute-start.13 = (bf16[1,64,128]{2,1,0:T(8,128)(2,1)S(1)}, bf16[1,64,128]{2,1,0:T(8,128)(2,1)S(1)}, u32[]{:S(2)}, u32[]{:S(2)}) collective-permute-start(bf16[1,64,128]{2,1,0:T(8,128)(2,1)S(1)} %bitcast.120), channel_id=1, source_target_pairs={{0,448},{32,480},{64,384},{96,416},{128,320},{160,352},{192,256},{... | collective-permute-start | bytes 49160 | tf_op jit(solution)/shard_map/ppermute | solution.py:35
  88.1 3.0 %collective-permute-start.14 = (bf16[1,64,128]{2,1,0:T(8,128)(2,1)S(1)}, bf16[1,64,128]{2,1,0:T(8,128)(2,1)S(1)}, u32[]{:S(2)}, u32[]{:S(2)}) collective-permute-start(bf16[1,64,128]{2,1,0:T(8,128)(2,1)S(1)} %bitcast.119), channel_id=1, source_target_pairs={{0,480},{32,448},{64,416},{96,384},{128,352},{160,320},{192,288},{... | collective-permute-start | bytes 49160 | tf_op jit(solution)/shard_map/ppermute | solution.py:35
  91.2 0.4 collective-permute-done.13
  91.6 2.7 %collective-permute-done.14 = bf16[1,64,128]{2,1,0:T(8,128)(2,1)S(1)} collective-permute-done((bf16[1,64,128]{2,1,0:T(8,128)(2,1)S(1)}, bf16[1,64,128]{2,1,0:T(8,128)(2,1)S(1)}, u32[]{:S(2)}, u32[]{:S(2)}) %collective-permute-start.14) | collective-permute-done | bytes 16416 | tf_op jit(solution)/shard_map/ppermute | solution.py:35
  94.4 0.6 gather_fusion.1
  95.0 0.1 fusion.45
  95.1 0.8 copy.68
  95.9 8.5 %fusion.2 = f32[64,32,256]{2,1,0:T(8,128)} fusion(bf16[32,32,64]{1,0,2:T(8,128)(2,1)S(1)} %copy.68, f32[256,32]{0,1:T(8,128)S(1)} %sqrt_add_fusion, f32[64]{0:T(128)S(1)} %convert_multiply_fusion.1), kind=kOutput, calls=%fused_computation.11 | convolution fusion | flops 34603008 | bytes 2261248 | tf_op jit(solution)/shard_map/fph,ghf->pfg/dot_general | solution.py:123
  104.4 6.9 %fusion.6 = f32[64,32,256]{2,1,0:T(8,128)S(1)} fusion(bf16[32,32,64]{1,0,2:T(8,128)(2,1)S(1)} %copy.68, f32[256,32]{0,1:T(8,128)S(1)} %sqrt_add_fusion, f32[64]{0:T(128)S(1)} %convert_multiply_fusion.1), kind=kOutput, calls=%fused_computation.12 | convolution fusion | flops 34603008 | bytes 2261248 | tf_op jit(solution)/shard_map/fph,ghf->pfg/dot_general | solution.py:120
  111.3 0.8 copy.69
  112.0 9.6 %add_bitcast_fusion = f32[256,64,32]{0,2,1:T(8,128)S(1)} fusion(f32[64,32,256]{2,1,0:T(8,128)} %fusion.2, bf16[32,32,64]{1,0,2:T(8,128)(2,1)S(1)} %copy.69, f32[256,32]{0,1:T(8,128)S(1)} %sqrt_add_fusion, f32[64]{0:T(128)S(1)} %convert_multiply_fusion.1), kind=kOutput, calls=%fused_computation.9 | convolution fusion | flops 35127296 | bytes 4358400 | tf_op jit(solution)/shard_map/fph,ghf->pfg/dot_general | solution.py:125
  121.6 7.0 %subtract_bitcast_fusion = f32[256,64,32]{0,2,1:T(8,128)S(1)} fusion(f32[64,32,256]{2,1,0:T(8,128)S(1)} %fusion.6, bf16[32,32,64]{1,0,2:T(8,128)(2,1)S(1)} %copy.69, f32[256,32]{0,1:T(8,128)S(1)} %sqrt_add_fusion, f32[64]{0:T(128)S(1)} %convert_multiply_fusion.1), kind=kOutput, calls=%fused_computation.10 | convolution fusion | flops 35127296 | bytes 4358400 | tf_op jit(solution)/shard_map/fph,ghf->pfg/dot_general | solution.py:122
  128.7 2.3 pad_maximum_fusion
  130.9 5.7 %copy.50 = f32[256,4096]{1,0:T(8,128)} copy(f32[256,4096]{0,1:T(8,128)} %bitcast.112) | data formatting | bytes 8388608
  136.6 0.0 reduce-scatter.7.cloned.1.call-update
  136.6 0.0 reduce-scatter.5.cloned.1.call-start
  136.7 54.8 %reduce-scatter.7.cloned.1.call-done = f32[64,4096]{1,0:T(8,128)} async-done(((f32[256,4096]{1,0:T(8,128)}), f32[64,4096]{1,0:T(8,128)}) %reduce-scatter.7.cloned.1.call-update) | async-done | bytes 1048592
  191.5 1.8 copy.51
  193.3 2.7 %copy.47 = f32[64,64,64]{2,1,0:T(8,128)} copy(f32[64,64,64]{0,2,1:T(8,128)S(1)} %bitcast.113) | data formatting | bytes 2097152 | tf_op jit(solution)/shard_map/reduce_scatter | solution.py:48
  196.0 47.5 %reduce-scatter.5.cloned.1.call-done = f32[8,64,64]{2,1,0:T(8,128)} async-done(((f32[64,64,64]{2,1,0:T(8,128)}), f32[8,64,64]{2,1,0:T(8,128)}) %reduce-scatter.5.cloned.1.call-update) | async-done | bytes 131088 | tf_op jit(solution)/shard_map/reduce_scatter | solution.py:48
  243.5 1.7 broadcast_multiply_fusion
  (57 shorter events, 0.4 us)
Async XLA Ops:
  6.5 1.0 copy-start
  11.8 18.4 %all-to-all-start = ((bf16[16,64,128]{2,1,0:T(8,128)(2,1)}), bf16[16,64,128]{2,1,0:T(8,128)(2,1)S(1)}, u32[]{:S(2)}, u32[]{:S(2)}) async-start(bf16[16,64,128]{2,1,0:T(8,128)(2,1)} %bitcast.1), calls=%async_computation | async-start | bytes 524288 | tf_op jit(solution)/shard_map/all_to_all | solution.py:99
  19.0 172.5 %reduce-scatter.7.cloned.1.call-start = ((), (), s32[]{:S(2)}) async-start(), calls=%async_computation.4 | async-start | bytes 5242880
  22.3 7.0 %copy-start.1 = (s32[256]{0:T(256)S(1)}, s32[256]{0:T(256)}, u32[]{:S(2)}) copy-start(s32[256]{0:T(256)} %param.7) | copy-start | bytes 3076
  36.2 15.0 %collective-permute-start = (bf16[1,64,128]{2,1,0:T(8,128)(2,1)S(1)}, bf16[1,64,128]{2,1,0:T(8,128)(2,1)S(1)}, u32[]{:S(2)}, u32[]{:S(2)}) collective-permute-start(bf16[1,64,128]{2,1,0:T(8,128)(2,1)S(1)} %bitcast.133), channel_id=1, source_target_pairs={{0,32},{32,0},{64,96},{96,64},{128,160},{160,128},{192,224},{224,1... | collective-permute-start | bytes 49160 | tf_op jit(solution)/shard_map/ppermute | solution.py:35
  39.0 16.4 %collective-permute-start.1 = (bf16[1,64,128]{2,1,0:T(8,128)(2,1)S(1)}, bf16[1,64,128]{2,1,0:T(8,128)(2,1)S(1)}, u32[]{:S(2)}, u32[]{:S(2)}) collective-permute-start(bf16[1,64,128]{2,1,0:T(8,128)(2,1)S(1)} %bitcast.132), channel_id=1, source_target_pairs={{0,64},{32,96},{64,0},{96,32},{128,192},{160,224},{192,128},{224,1... | collective-permute-start | bytes 49160 | tf_op jit(solution)/shard_map/ppermute | solution.py:35
  41.3 16.9 %collective-permute-start.2 = (bf16[1,64,128]{2,1,0:T(8,128)(2,1)S(1)}, bf16[1,64,128]{2,1,0:T(8,128)(2,1)S(1)}, u32[]{:S(2)}, u32[]{:S(2)}) collective-permute-start(bf16[1,64,128]{2,1,0:T(8,128)(2,1)S(1)} %bitcast.131), channel_id=1, source_target_pairs={{0,96},{32,64},{64,32},{96,0},{128,224},{160,192},{192,160},{224,1... | collective-permute-start | bytes 49160 | tf_op jit(solution)/shard_map/ppermute | solution.py:35
  44.2 20.7 %collective-permute-start.3 = (bf16[1,64,128]{2,1,0:T(8,128)(2,1)S(1)}, bf16[1,64,128]{2,1,0:T(8,128)(2,1)S(1)}, u32[]{:S(2)}, u32[]{:S(2)}) collective-permute-start(bf16[1,64,128]{2,1,0:T(8,128)(2,1)S(1)} %bitcast.130), channel_id=1, source_target_pairs={{0,128},{32,160},{64,192},{96,224},{128,0},{160,32},{192,64},{224,... | collective-permute-start | bytes 49160 | tf_op jit(solution)/shard_map/ppermute | solution.py:35
  47.8 20.3 %collective-permute-start.4 = (bf16[1,64,128]{2,1,0:T(8,128)(2,1)S(1)}, bf16[1,64,128]{2,1,0:T(8,128)(2,1)S(1)}, u32[]{:S(2)}, u32[]{:S(2)}) collective-permute-start(bf16[1,64,128]{2,1,0:T(8,128)(2,1)S(1)} %bitcast.129), channel_id=1, source_target_pairs={{0,160},{32,128},{64,224},{96,192},{128,32},{160,0},{192,96},{224,... | collective-permute-start | bytes 49160 | tf_op jit(solution)/shard_map/ppermute | solution.py:35
  51.2 20.5 %collective-permute-start.5 = (bf16[1,64,128]{2,1,0:T(8,128)(2,1)S(1)}, bf16[1,64,128]{2,1,0:T(8,128)(2,1)S(1)}, u32[]{:S(2)}, u32[]{:S(2)}) collective-permute-start(bf16[1,64,128]{2,1,0:T(8,128)(2,1)S(1)} %bitcast.128), channel_id=1, source_target_pairs={{0,192},{32,224},{64,128},{96,160},{128,64},{160,96},{192,0},{224,... | collective-permute-start | bytes 49160 | tf_op jit(solution)/shard_map/ppermute | solution.py:35
  55.4 21.0 %collective-permute-start.6 = (bf16[1,64,128]{2,1,0:T(8,128)(2,1)S(1)}, bf16[1,64,128]{2,1,0:T(8,128)(2,1)S(1)}, u32[]{:S(2)}, u32[]{:S(2)}) collective-permute-start(bf16[1,64,128]{2,1,0:T(8,128)(2,1)S(1)} %bitcast.127), channel_id=1, source_target_pairs={{0,224},{32,192},{64,160},{96,128},{128,96},{160,64},{192,32},{224... | collective-permute-start | bytes 49160 | tf_op jit(solution)/shard_map/ppermute | solution.py:35
  58.2 21.2 %collective-permute-start.7 = (bf16[1,64,128]{2,1,0:T(8,128)(2,1)S(1)}, bf16[1,64,128]{2,1,0:T(8,128)(2,1)S(1)}, u32[]{:S(2)}, u32[]{:S(2)}) collective-permute-start(bf16[1,64,128]{2,1,0:T(8,128)(2,1)S(1)} %bitcast.126), channel_id=1, source_target_pairs={{0,256},{32,288},{64,320},{96,352},{128,384},{160,416},{192,448},{... | collective-permute-start | bytes 49160 | tf_op jit(solution)/shard_map/ppermute | solution.py:35
  64.9 19.6 %collective-permute-start.8 = (bf16[1,64,128]{2,1,0:T(8,128)(2,1)S(1)}, bf16[1,64,128]{2,1,0:T(8,128)(2,1)S(1)}, u32[]{:S(2)}, u32[]{:S(2)}) collective-permute-start(bf16[1,64,128]{2,1,0:T(8,128)(2,1)S(1)} %bitcast.125), channel_id=1, source_target_pairs={{0,288},{32,256},{64,352},{96,320},{128,416},{160,384},{192,480},{... | collective-permute-start | bytes 49160 | tf_op jit(solution)/shard_map/ppermute | solution.py:35
  68.2 19.9 %collective-permute-start.9 = (bf16[1,64,128]{2,1,0:T(8,128)(2,1)S(1)}, bf16[1,64,128]{2,1,0:T(8,128)(2,1)S(1)}, u32[]{:S(2)}, u32[]{:S(2)}) collective-permute-start(bf16[1,64,128]{2,1,0:T(8,128)(2,1)S(1)} %bitcast.124), channel_id=1, source_target_pairs={{0,320},{32,352},{64,256},{96,288},{128,448},{160,480},{192,384},{... | collective-permute-start | bytes 49160 | tf_op jit(solution)/shard_map/ppermute | solution.py:35
  71.7 19.4 %collective-permute-start.10 = (bf16[1,64,128]{2,1,0:T(8,128)(2,1)S(1)}, bf16[1,64,128]{2,1,0:T(8,128)(2,1)S(1)}, u32[]{:S(2)}, u32[]{:S(2)}) collective-permute-start(bf16[1,64,128]{2,1,0:T(8,128)(2,1)S(1)} %bitcast.123), channel_id=1, source_target_pairs={{0,352},{32,320},{64,288},{96,256},{128,480},{160,448},{192,416},{... | collective-permute-start | bytes 49160 | tf_op jit(solution)/shard_map/ppermute | solution.py:35
  76.4 14.8 %collective-permute-start.11 = (bf16[1,64,128]{2,1,0:T(8,128)(2,1)S(1)}, bf16[1,64,128]{2,1,0:T(8,128)(2,1)S(1)}, u32[]{:S(2)}, u32[]{:S(2)}) collective-permute-start(bf16[1,64,128]{2,1,0:T(8,128)(2,1)S(1)} %bitcast.122), channel_id=1, source_target_pairs={{0,384},{32,416},{64,448},{96,480},{128,256},{160,288},{192,320},{... | collective-permute-start | bytes 49160 | tf_op jit(solution)/shard_map/ppermute | solution.py:35
  79.5 11.7 %collective-permute-start.12 = (bf16[1,64,128]{2,1,0:T(8,128)(2,1)S(1)}, bf16[1,64,128]{2,1,0:T(8,128)(2,1)S(1)}, u32[]{:S(2)}, u32[]{:S(2)}) collective-permute-start(bf16[1,64,128]{2,1,0:T(8,128)(2,1)S(1)} %bitcast.121), channel_id=1, source_target_pairs={{0,416},{32,384},{64,480},{96,448},{128,288},{160,256},{192,352},{... | collective-permute-start | bytes 49160 | tf_op jit(solution)/shard_map/ppermute | solution.py:35
  84.5 7.1 %collective-permute-start.13 = (bf16[1,64,128]{2,1,0:T(8,128)(2,1)S(1)}, bf16[1,64,128]{2,1,0:T(8,128)(2,1)S(1)}, u32[]{:S(2)}, u32[]{:S(2)}) collective-permute-start(bf16[1,64,128]{2,1,0:T(8,128)(2,1)S(1)} %bitcast.120), channel_id=1, source_target_pairs={{0,448},{32,480},{64,384},{96,416},{128,320},{160,352},{192,256},{... | collective-permute-start | bytes 49160 | tf_op jit(solution)/shard_map/ppermute | solution.py:35
  88.1 6.3 %collective-permute-start.14 = (bf16[1,64,128]{2,1,0:T(8,128)(2,1)S(1)}, bf16[1,64,128]{2,1,0:T(8,128)(2,1)S(1)}, u32[]{:S(2)}, u32[]{:S(2)}) collective-permute-start(bf16[1,64,128]{2,1,0:T(8,128)(2,1)S(1)} %bitcast.119), channel_id=1, source_target_pairs={{0,480},{32,448},{64,416},{96,384},{128,352},{160,320},{192,288},{... | collective-permute-start | bytes 49160 | tf_op jit(solution)/shard_map/ppermute | solution.py:35
  136.6 106.9 %reduce-scatter.5.cloned.1.call-start = ((), (), s32[]{:S(2)}) async-start(), calls=%async_computation.3 | async-start | bytes 2359296 | tf_op jit(solution)/shard_map/reduce_scatter | solution.py:48
Sparse Core Ops, SparseCore 0:
  136.8 54.6 reduce-scatter.6
  196.2 47.3 reduce-scatter.4
